TPU v7x, 32 devices: a whole 2x2x4 slice. The times are simulated.
32 devices in a mesh: dp: 2 (over x), context: 4 (over y, core), tensor: 4 (over z).
Axes of the slice: x: 2, y: 2, z: 4, core: 2. Of those that a mesh axis runs over, the one named last changes fastest.
Arguments:
- hidden_in: bfloat16 [16, 1024, 576], P('dp', ('context', 'tensor')), may hold values from -6 to 6
- attn_gain: bfloat16 [576], P('dp'), may hold values from 0.099609375 to 1.8984375
- query_weight: bfloat16 [576, 576], P('dp'), may hold values from -0.25 to 0.25
- key_weight: bfloat16 [576, 192], P('dp'), may hold values from -0.25 to 0.25
- value_weight: bfloat16 [576, 192], P('dp'), may hold values from -0.25 to 0.25
- output_weight: bfloat16 [576, 576], P('dp'), may hold values from -3 to 3
- ffn_gain: bfloat16 [576], P('dp'), may hold values from 0.099609375 to 1.8984375
- gate_weight: bfloat16 [576, 1536], P('dp', 'tensor'), may hold values from -0.25 to 0.25
- up_weight: bfloat16 [576, 1536], P('dp', 'tensor'), may hold values from -0.25 to 0.25
- down_weight: bfloat16 [1536, 576], P('tensor', 'dp'), may hold values from -0.15625 to 0.15625
- out_grad: bfloat16 [16, 1024, 576], P('dp', ('context', 'tensor')), may hold values from -6 to 6
Outputs:
- hidden_out: bfloat16 [16, 1024, 576], P('dp', ('context', 'tensor'))
- input_grad: float32 [16, 1024, 576], P('dp', ('context', 'tensor'))
- attn_gain_grad: float32 [576], P('dp')
- query_weight_grad: float32 [576, 576], P('dp')
- key_weight_grad: float32 [576, 192], P('dp')
- value_weight_grad: float32 [576, 192], P('dp')
- output_weight_grad: float32 [576, 576], P('dp')
- ffn_gain_grad: float32 [576], P('dp')
- gate_weight_grad: float32 [576, 1536], P('dp', 'tensor')
- up_weight_grad: float32 [576, 1536], P('dp', 'tensor')
- down_weight_grad: float32 [1536, 576], P('tensor', 'dp')
All inputs are finite; a program needn't handle non-finite values.
Results may differ from a plain program's by a relative error of at most 0.024.
Values may be sent and summed in bfloat16 or wider, within the bound.
No kernel may reach another device: no remote copies, remote signals or barrier semaphores. Data moves between devices by JAX's collectives and lax.ppermute only.
A program may use at most 128 MiB of HBM per device.

v0:
```python
import jax
import jax.numpy as jnp
from jax import lax
from jax.sharding import PartitionSpec as P

HEADS = 9
KV_HEADS = 3
HEAD_DIM = 64
EPS = 1e-05
ROPE_BASE = 100000.0


def rotary(places, half_dim):
    frequency = ROPE_BASE ** (-jnp.arange(half_dim).astype(jnp.float32) / half_dim)
    angles = places.astype(jnp.float32)[:, None] * frequency[None, :]
    return (jnp.cos(angles), jnp.sin(angles))


def rotate(tensor, cosine_table, sine_table):
    half_dim = tensor.shape[-1] // 2
    first_half = tensor[..., :half_dim]
    second_half = tensor[..., half_dim:]
    cosine_b = cosine_table[:, None, :]
    sine_b = sine_table[:, None, :]
    return jnp.concatenate(
        [
            first_half * cosine_b - second_half * sine_b,
            second_half * cosine_b + first_half * sine_b,
        ],
        axis=-1,
    )


def rotate_back(tensor, cosine_table, sine_table):
    half_dim = tensor.shape[-1] // 2
    first_half = tensor[..., :half_dim]
    second_half = tensor[..., half_dim:]
    cosine_b = cosine_table[:, None, :]
    sine_b = sine_table[:, None, :]
    return jnp.concatenate(
        [
            first_half * cosine_b + second_half * sine_b,
            second_half * cosine_b - first_half * sine_b,
        ],
        axis=-1,
    )


def times_transposed(left, right):
    return lax.dot_general(
        left, right, (((1,), (1,)), ((), ())), preferred_element_type=jnp.float32
    )


def transposed_times(left, right):
    return lax.dot_general(
        left, right, (((0,), (0,)), ((), ())), preferred_element_type=jnp.float32
    )


def norm_back(grad_normed, normed, inverse):
    return inverse * (grad_normed - normed * jnp.mean(grad_normed * normed, axis=-1, keepdims=True))


def body(
    hidden_in,
    attn_gain,
    query_weight,
    key_weight,
    value_weight,
    output_weight,
    ffn_gain,
    gate_weight,
    up_weight,
    down_weight,
    out_grad,
):
    seq_count, local_len, model_width = hidden_in.shape
    kv_width = KV_HEADS * HEAD_DIM
    repeat = HEADS // KV_HEADS
    scale = HEAD_DIM ** (-0.5)
    token_rows = seq_count * local_len
    gain_one, query_all, key_all, value_all, output_all = (
        lax.all_gather(attn_gain, "dp", axis=0, tiled=True),
        lax.all_gather(query_weight, "dp", axis=0, tiled=True),
        lax.all_gather(key_weight, "dp", axis=0, tiled=True),
        lax.all_gather(value_weight, "dp", axis=0, tiled=True),
        lax.all_gather(output_weight, "dp", axis=0, tiled=True),
    )
    gain_two, gate_all, up_all, down_all = (
        lax.all_gather(ffn_gain, "dp", axis=0, tiled=True),
        lax.all_gather(gate_weight, "dp", axis=0, tiled=True),
        lax.all_gather(up_weight, "dp", axis=0, tiled=True),
        lax.all_gather(down_weight, "dp", axis=1, tiled=True),
    )
    places = lax.axis_index(("context", "tensor")) * local_len + jnp.arange(
        local_len, dtype=jnp.int32
    )
    cosine_table, sine_table = rotary(places, HEAD_DIM // 2)
    rows_in = hidden_in.astype(jnp.float32)
    inverse_one = lax.rsqrt(jnp.mean(rows_in * rows_in, axis=-1, keepdims=True) + EPS)
    normed_one = rows_in * inverse_one
    normed_low = (normed_one * gain_one.astype(jnp.float32)).astype(jnp.bfloat16)
    flat_normed = normed_low.reshape(token_rows, model_width)
    queries = jnp.dot(flat_normed, query_all, preferred_element_type=jnp.float32).reshape(
        seq_count, local_len, HEADS, HEAD_DIM
    )
    key_rows = jnp.dot(flat_normed, key_all, preferred_element_type=jnp.float32).reshape(
        seq_count, local_len, KV_HEADS, HEAD_DIM
    )
    value_rows = jnp.dot(flat_normed, value_all, preferred_element_type=jnp.float32).reshape(
        seq_count, local_len, kv_width
    )
    queries_low = rotate(queries, cosine_table, sine_table).astype(jnp.bfloat16)
    keys_low = (
        rotate(key_rows, cosine_table, sine_table)
        .astype(jnp.bfloat16)
        .reshape(seq_count, local_len, kv_width)
    )
    kv_local = jnp.concatenate([keys_low, value_rows.astype(jnp.bfloat16)], axis=-1)
    kv_whole = lax.all_gather(kv_local, ("context", "tensor"), axis=1, tiled=True)
    seq_len = kv_whole.shape[1]
    query_groups = queries_low.reshape(seq_count, local_len, KV_HEADS, repeat, HEAD_DIM)

    def attend_one(operands):
        query_seq, kv_seq = operands
        key_seq = kv_seq[:, :kv_width].reshape(seq_len, KV_HEADS, HEAD_DIM)
        value_seq = kv_seq[:, kv_width:].reshape(seq_len, KV_HEADS, HEAD_DIM)
        scores = (
            jnp.einsum("qgre,kge->grqk", query_seq, key_seq, preferred_element_type=jnp.float32)
            * scale
        )
        allowed = jnp.arange(seq_len)[None, :] <= places[:, None]
        scores = jnp.where(allowed, scores, -1e30)
        row_max = jnp.max(scores, axis=-1, keepdims=True)
        weights = jnp.exp(scores - row_max)
        row_sum = jnp.sum(weights, axis=-1, keepdims=True)
        probability = (weights / row_sum).astype(jnp.bfloat16)
        attended_seq = jnp.einsum(
            "grqk,kge->qgre", probability, value_seq, preferred_element_type=jnp.float32
        )
        return (
            attended_seq.reshape(local_len, HEADS * HEAD_DIM),
            row_max[..., 0] + jnp.log(row_sum[..., 0]),
        )

    attended, log_sums = lax.map(attend_one, (query_groups, kv_whole))
    attended_low = attended.astype(jnp.bfloat16)
    attended_flat = attended_low.reshape(token_rows, HEADS * HEAD_DIM)
    middle = rows_in + jnp.dot(
        attended_flat, output_all, preferred_element_type=jnp.float32
    ).reshape(seq_count, local_len, model_width)
    inverse_two = lax.rsqrt(jnp.mean(middle * middle, axis=-1, keepdims=True) + EPS)
    normed_two = middle * inverse_two
    ffn_low = (normed_two * gain_two.astype(jnp.float32)).astype(jnp.bfloat16)
    ffn_rows = lax.all_gather(ffn_low, "tensor", axis=1, tiled=True)
    block_len = ffn_rows.shape[1]
    wide_rows = seq_count * block_len
    flat_rows = ffn_rows.reshape(wide_rows, model_width)
    gate_act = jnp.dot(flat_rows, gate_all, preferred_element_type=jnp.float32)
    up_act = jnp.dot(flat_rows, up_all, preferred_element_type=jnp.float32)
    sigmoid_gate = jax.nn.sigmoid(gate_act)
    silu_act = gate_act * sigmoid_gate
    hidden_low = (silu_act * up_act).astype(jnp.bfloat16)
    partial_out = jnp.dot(hidden_low, down_all, preferred_element_type=jnp.float32).reshape(
        seq_count, block_len, model_width
    )
    ffn_out = lax.psum_scatter(
        partial_out.astype(jnp.bfloat16), "tensor", scatter_dimension=1, tiled=True
    ).astype(jnp.float32)
    hidden_out = (middle + ffn_out).astype(jnp.bfloat16)
    grad_rows = lax.all_gather(out_grad, "tensor", axis=1, tiled=True).reshape(
        wide_rows, model_width
    )
    grad_hidden = times_transposed(grad_rows, down_all)
    down_grad = transposed_times(hidden_low, grad_rows)
    grad_up_low = (grad_hidden * silu_act).astype(jnp.bfloat16)
    grad_gate_low = (
        grad_hidden * up_act * (sigmoid_gate * (1.0 + gate_act * (1.0 - sigmoid_gate)))
    ).astype(jnp.bfloat16)
    gate_grad = transposed_times(flat_rows, grad_gate_low)
    up_grad = transposed_times(flat_rows, grad_up_low)
    grad_ffn_part = (
        times_transposed(grad_gate_low, gate_all) + times_transposed(grad_up_low, up_all)
    ).reshape(seq_count, block_len, model_width)
    grad_ffn_in = lax.psum_scatter(
        grad_ffn_part.astype(jnp.bfloat16), "tensor", scatter_dimension=1, tiled=True
    ).astype(jnp.float32)
    ffn_gain_term = jnp.sum(grad_ffn_in * normed_two, axis=(0, 1))
    grad_middle = out_grad.astype(jnp.float32) + norm_back(
        grad_ffn_in * gain_two.astype(jnp.float32), normed_two, inverse_two
    )
    grad_mid_low = grad_middle.astype(jnp.bfloat16).reshape(token_rows, model_width)
    out_proj_grad = transposed_times(attended_flat, grad_mid_low)
    grad_attended = (
        times_transposed(grad_mid_low, output_all)
        .astype(jnp.bfloat16)
        .reshape(seq_count, local_len, KV_HEADS, repeat, HEAD_DIM)
    )
    attended_groups = attended.reshape(seq_count, local_len, KV_HEADS, repeat, HEAD_DIM)
    row_delta = jnp.transpose(
        jnp.sum(grad_attended.astype(jnp.float32) * attended_groups, axis=-1), (0, 2, 3, 1)
    )
    piece = lax.all_gather(kv_local, ("context", "tensor"), axis=1, tiled=True)
    piece_len = piece.shape[1]
    key_piece = piece[..., :kv_width].reshape(seq_count, piece_len, KV_HEADS, HEAD_DIM)
    value_piece = piece[..., kv_width:].reshape(seq_count, piece_len, KV_HEADS, HEAD_DIM)
    scores = (
        jnp.einsum("sqgre,skge->sgrqk", query_groups, key_piece, preferred_element_type=jnp.float32)
        * scale
    )
    allowed = jnp.arange(piece_len)[None, :] <= places[:, None]
    probs_full = jnp.exp(jnp.where(allowed, scores - log_sums[..., None], -1e30))
    grad_probs = jnp.einsum(
        "sqgre,skge->sgrqk", grad_attended, value_piece, preferred_element_type=jnp.float32
    )
    grad_scores = (probs_full * (grad_probs - row_delta[..., None])).astype(jnp.bfloat16)
    key_piece, probs_full, grad_scores = (key_piece, probs_full, grad_scores)
    grad_query = (
        jnp.einsum("sgrqk,skge->sqgre", grad_scores, key_piece, preferred_element_type=jnp.float32)
        * scale
    )
    piece_len = piece.shape[1]
    grad_keys = (
        jnp.einsum(
            "sgrqk,sqgre->skge", grad_scores, query_groups, preferred_element_type=jnp.float32
        )
        * scale
    )
    grad_values = jnp.einsum(
        "sgrqk,sqgre->skge",
        probs_full.astype(jnp.bfloat16),
        grad_attended,
        preferred_element_type=jnp.float32,
    )
    grad_piece = jnp.concatenate(
        [
            grad_keys.reshape(seq_count, piece_len, kv_width),
            grad_values.reshape(seq_count, piece_len, kv_width),
        ],
        axis=-1,
    )
    grad_kv = grad_piece
    grad_query, grad_kv = (grad_query, grad_kv)
    grad_kv_own = lax.psum_scatter(
        grad_kv.astype(jnp.bfloat16), ("context", "tensor"), scatter_dimension=1, tiled=True
    ).astype(jnp.float32)
    grad_keys_low = (
        rotate_back(
            grad_kv_own[..., :kv_width].reshape(seq_count, local_len, KV_HEADS, HEAD_DIM),
            cosine_table,
            sine_table,
        )
        .astype(jnp.bfloat16)
        .reshape(token_rows, kv_width)
    )
    grad_values_low = grad_kv_own[..., kv_width:].astype(jnp.bfloat16).reshape(token_rows, kv_width)
    grad_query_low = (
        rotate_back(
            grad_query.reshape(seq_count, local_len, HEADS, HEAD_DIM), cosine_table, sine_table
        )
        .astype(jnp.bfloat16)
        .reshape(token_rows, HEADS * HEAD_DIM)
    )
    query_grad = transposed_times(flat_normed, grad_query_low)
    key_grad = transposed_times(flat_normed, grad_keys_low)
    value_grad = transposed_times(flat_normed, grad_values_low)
    grad_normed = (
        times_transposed(grad_query_low, query_all)
        + times_transposed(grad_keys_low, key_all)
        + times_transposed(grad_values_low, value_all)
    )
    grad_normed = grad_normed.reshape(seq_count, local_len, model_width)
    attn_gain_term = jnp.sum(grad_normed * normed_one, axis=(0, 1))
    input_grad = grad_middle + norm_back(
        grad_normed * gain_one.astype(jnp.float32), normed_one, inverse_one
    )
    shards = (
        lax.psum_scatter(
            attn_gain_term.astype(jnp.bfloat16), "dp", scatter_dimension=0, tiled=True
        ).astype(jnp.float32),
        lax.psum_scatter(
            ffn_gain_term.astype(jnp.bfloat16), "dp", scatter_dimension=0, tiled=True
        ).astype(jnp.float32),
        lax.psum_scatter(
            query_grad.astype(jnp.bfloat16), "dp", scatter_dimension=0, tiled=True
        ).astype(jnp.float32),
        lax.psum_scatter(
            key_grad.astype(jnp.bfloat16), "dp", scatter_dimension=0, tiled=True
        ).astype(jnp.float32),
        lax.psum_scatter(
            value_grad.astype(jnp.bfloat16), "dp", scatter_dimension=0, tiled=True
        ).astype(jnp.float32),
        lax.psum_scatter(
            out_proj_grad.astype(jnp.bfloat16), "dp", scatter_dimension=0, tiled=True
        ).astype(jnp.float32),
        lax.psum_scatter(
            gate_grad.astype(jnp.bfloat16), "dp", scatter_dimension=0, tiled=True
        ).astype(jnp.float32),
        lax.psum_scatter(
            up_grad.astype(jnp.bfloat16), "dp", scatter_dimension=0, tiled=True
        ).astype(jnp.float32),
        lax.psum_scatter(
            down_grad.astype(jnp.bfloat16), "dp", scatter_dimension=1, tiled=True
        ).astype(jnp.float32),
    )
    attn_sums = (
        lax.psum(shards[0].astype(jnp.bfloat16), ("context", "tensor")).astype(jnp.float32),
        lax.psum(shards[1].astype(jnp.bfloat16), ("context", "tensor")).astype(jnp.float32),
        lax.psum(shards[2].astype(jnp.bfloat16), ("context", "tensor")).astype(jnp.float32),
        lax.psum(shards[3].astype(jnp.bfloat16), ("context", "tensor")).astype(jnp.float32),
        lax.psum(shards[4].astype(jnp.bfloat16), ("context", "tensor")).astype(jnp.float32),
        lax.psum(shards[5].astype(jnp.bfloat16), ("context", "tensor")).astype(jnp.float32),
    )
    ffn_sums = (
        lax.psum(shards[6].astype(jnp.bfloat16), "context").astype(jnp.float32),
        lax.psum(shards[7].astype(jnp.bfloat16), "context").astype(jnp.float32),
        lax.psum(shards[8].astype(jnp.bfloat16), "context").astype(jnp.float32),
    )
    return (
        hidden_out,
        input_grad,
        attn_sums[0],
        attn_sums[2],
        attn_sums[3],
        attn_sums[4],
        attn_sums[5],
        attn_sums[1],
        ffn_sums[0],
        ffn_sums[1],
        ffn_sums[2],
    )


def solution(mesh):
    placed = (
        P("dp", ("context", "tensor"), None),
        P("dp"),
        P("dp", None),
        P("dp", None),
        P("dp", None),
        P("dp", None),
        P("dp"),
        P("dp", "tensor"),
        P("dp", "tensor"),
        P("tensor", "dp"),
        P("dp", ("context", "tensor"), None),
    )
    return jax.shard_map(
        body,
        mesh=mesh,
        in_specs=placed,
        out_specs=(
            P("dp", ("context", "tensor"), None),
            P("dp", ("context", "tensor"), None),
            P("dp"),
            P("dp", None),
            P("dp", None),
            P("dp", None),
            P("dp", None),
            P("dp"),
            P("dp", "tensor"),
            P("dp", "tensor"),
            P("tensor", "dp"),
        ),
        check_vma=False,
    )
```

profile of v0, /device:TPU:0, one launch (start us, length us, event | category | flops | bytes accessed | tf_op | source)
XLA Modules:
  0.0 730.7 jit_solution(6010033176116477348)
XLA Ops:
  11.0 5.8 all-reduce.8
  18.2 6.1 all_gather.38
  25.0 6.0 all_gather.39
  33.8 8.2 %all_gather.41 = bf16[576,576]{1,0:T(8,128)(2,1)S(1)} all-gather(bf16[288,576]{1,0:T(8,128)(2,1)S(1)} %copy-done.29), channel_id=1, replica_groups=mesh['dp'=2,'context'=4,'tensor'=4] {'dp'}, dimensions={0}, use_global_device_ids=true | all-gather | bytes 995328 | tf_op jit(solution)/shard_map/all_gather | solution.py:85
  47.8 8.3 %all_gather.42 = bf16[576,576]{1,0:T(8,128)(2,1)} all-gather(bf16[288,576]{1,0:T(8,128)(2,1)S(1)} %copy-done.30), channel_id=1, replica_groups=mesh['dp'=2,'context'=4,'tensor'=4] {'dp'}, dimensions={0}, use_global_device_ids=true | all-gather | bytes 995328 | tf_op jit(solution)/shard_map/all_gather | solution.py:88
  56.1 40.9 %all-gather.4.cloned.1.call-done = bf16[8,1024,384]{2,1,0:T(8,128)(2,1)} async-done(((bf16[8,64,384]{2,1,0:T(8,128)(2,1)}), bf16[8,1024,384]{2,1,0:T(8,128)(2,1)}) %all-gather.4.cloned.1.call-update) | async-done | bytes 6291472 | tf_op jit(solution)/shard_map/all_gather | solution.py:121
  97.0 41.1 %while.13 = (s32[]{:T(128)}, f32[8,64,576]{1,2,0:T(8,128)}, f32[8,3,3,64]{3,2,1,0:T(4,128)}, bf16[8,1024,384]{2,1,0:T(8,128)(2,1)}, bf16[8,64,3,3,64]{4,1,3,2,0:T(8,128)(2,1)S(1)}, /*index=5*/s32[]{:T(128)}, s32[]{:T(128)}) while((s32[]{:T(128)}, f32[8,64,576]{1,2,0:T(8,128)}, f32[8,3,3,64]{3,2,1,0:T(4,128)}, ...), condition=%wide.region_4.5_spmd.clone, body=%wide.region_1.4_spmd.clone.sunk | while | flops 158137856 | bytes 13605225 | solution.py:147
  138.1 3.2 multiply_reduce_fusion
  144.2 8.4 %all_gather.45 = bf16[576,384]{1,0:T(8,128)(2,1)} all-gather(bf16[288,384]{1,0:T(8,128)(2,1)S(1)} %copy-done.31), channel_id=1, replica_groups=mesh['dp'=2,'context'=4,'tensor'=4] {'dp'}, dimensions={0}, use_global_device_ids=true | all-gather | bytes 663552 | tf_op jit(solution)/shard_map/all_gather | solution.py:92
  152.6 7.5 %all_gather.46 = bf16[576,384]{1,0:T(8,128)(2,1)} all-gather(bf16[288,384]{1,0:T(8,128)(2,1)S(1)} %copy-done.32), channel_id=1, replica_groups=mesh['dp'=2,'context'=4,'tensor'=4] {'dp'}, dimensions={0}, use_global_device_ids=true | all-gather | bytes 663552 | tf_op jit(solution)/shard_map/all_gather | solution.py:93
  160.1 6.9 all_gather.47
  166.9 30.1 %all-gather.6.cloned.1.call-done = bf16[8,256,576]{2,1,0:T(8,128)(2,1)} async-done(((bf16[8,64,576]{2,1,0:T(8,128)(2,1)}), bf16[8,256,576]{2,1,0:T(8,128)(2,1)}) %all-gather.6.cloned.1.call-update) | async-done | bytes 2359312 | tf_op jit(solution)/shard_map/all_gather | solution.py:156
  197.0 3.6 fusion.65
  200.7 3.4 fusion.64
  204.1 48.1 %all-gather.8.cloned.1.call-done = bf16[8,256,576]{2,1,0:T(8,128)(2,1)} async-done(((bf16[8,64,576]{2,1,0:T(8,128)(2,1)}), bf16[8,256,576]{2,1,0:T(8,128)(2,1)}) %all-gather.8.cloned.1.call-update) | async-done | bytes 2359312 | tf_op jit(solution)/shard_map/all_gather | solution.py:172
  252.2 6.8 multiply_convert_fusion
  262.0 2.6 copy.73
  266.3 3.6 convolution_convert_fusion.3
  270.2 6.6 fusion.62
  276.8 6.3 copy.75
  283.1 5.0 copy.74
  288.1 4.4 convolution_convert_fusion.5
  292.6 9.3 %fusion.67 = f32[8,3,1024,64,3]{2,3,4,1,0:T(8,128)} fusion(bf16[8,1024,3,64,1]{1,3,4,2,0:T(8,128)(2,1)S(1)} %bitcast.200, bf16[8,64,3,3,64]{4,1,3,2,0:T(8,128)(2,1)} %copy-done.6), kind=kOutput, calls=%fused_computation.125 | convolution fusion | flops 603979776 | bytes 22609920 | tf_op jit(solution)/shard_map/sqgre,skge->sgrqk/dot_general | solution.py:209
  304.1 11.7 %reduce-scatter.13.cloned.1.call-done = bf16[8,64,576]{2,1,0:T(8,128)(2,1)} async-done(((bf16[8,256,576]{2,1,0:T(8,128)(2,1)}), bf16[8,64,576]{2,1,0:T(8,128)(2,1)}) %reduce-scatter.13.cloned.1.call-update) | async-done | bytes 589840 | tf_op jit(solution)/shard_map/reduce_scatter | solution.py:186
  315.8 2.2 fusion.37
  321.9 2.9 reshape.243
  324.8 3.6 fusion.26
  328.4 10.1 %bitcast_convert_fusion = bf16[8,3,64,1024]{3,2,1,0:T(8,128)(2,1)} fusion(f32[8,3,1024,64,3]{2,3,4,1,0:T(8,128)} %fusion.67, f32[8,3,3,64]{3,2,1,0:T(4,128)S(1)} %copy-done.39, pred[64,1024]{1,0:T(8,128)(4,1)S(1)} %iota_compare_fusion.1, bf16[8,64,3,3,64]{1,0,4,3,2:T(8,128)(2,1)S(1)} %copy-done.18), kind=kOutput, calls=%fused_computation.31 | convolution fusion | flops 624427008 | bytes 22693888 | tf_op jit(solution)/shard_map/sgrqk,sqgre->skge/dot_general | solution.py:230
  338.5 6.2 copy.83
  344.6 11.8 %fusion.12 = bf16[8,3,3,64,1024]{4,3,2,1,0:T(8,128)(2,1)S(1)} fusion(f32[8,3,1024,64,3]{2,3,4,1,0:T(8,128)} %fusion.67, f32[8,3,3,64]{3,2,1,0:T(4,128)S(1)} %copy.78, f32[8,3,3,64]{3,2,1,0:T(4,128)S(1)} %copy-done.39, pred[64,1024]{1,0:T(8,128)(4,1)S(1)} %iota_compare_fusion.1, bf16[8,1024,3,64,1]{1,3,4,2,0:T(8,128)(2,1)} %bitcast.218, ...), kind=kOutput, calls=%fused_computation.20 | convolution fusion | flops 632291328 | bytes 32149504 | tf_op jit(solution)/shard_map/sqgre,skge->sgrqk/dot_general | solution.py:214
  356.5 4.1 fusion.22
  361.1 6.2 copy.82
  367.2 8.3 %pad_maximum_fusion = bf16[8,1024,384]{2,1,0:T(8,128)(2,1)} fusion(bf16[8,1024,192]{2,1,0:T(8,128)(2,1)} %copy.83, bf16[8,1024,192]{2,1,0:T(8,128)(2,1)} %copy.82), kind=kLoop, calls=%fused_computation.30 | loop fusion | flops 12582912 | bytes 12582912 | tf_op jit(solution)/shard_map/concatenate | solution.py:236
  376.5 3.4 bitcast_convert_fusion.1
  380.0 6.3 convolution_multiply_fusion
  390.1 70.2 %reduce-scatter.15.cloned.1.call-done = bf16[8,64,384]{2,1,0:T(8,128)(2,1)} async-done(((bf16[8,1024,384]{2,1,0:T(8,128)(2,1)}), bf16[8,64,384]{2,1,0:T(8,128)(2,1)}) %reduce-scatter.15.cloned.1.call-update) | async-done | bytes 393232 | tf_op jit(solution)/shard_map/reduce_scatter | solution.py:245
  465.7 2.9 convolution_convert_fusion
  468.7 2.6 copy.72
  472.1 24.2 %all-reduce.14.cloned.1.call-done = (bf16[288,384]{1,0:T(8,128)(2,1)}, bf16[288,384]{1,0:T(8,128)(2,1)}, bf16[384,288]{0,1:T(8,128)(2,1)}) async-done(((bf16[288,384]{1,0:T(8,128)(2,1)}, bf16[288,384]{1,0:T(8,128)(2,1)}, bf16[384,288]{0,1:T(8,128)(2,1)}), (bf16[288,384]{1,0:T(8,128)(2,1)}, bf16[288,384]{1,0:T(8,128)(2,1)}, bf16[384,288]{0,1:T(8,128)(2,1)})) %all-reduce.14.cloned.1.call-update) | async-done | bytes 663568 | tf_op jit(solution)/shard_map/psum | solution.py:316
  507.0 8.8 %reduce-scatter.23.cloned.1.call-done = bf16[288,576]{1,0:T(8,128)(2,1)} async-done(((bf16[576,576]{1,0:T(8,128)(2,1)}), bf16[288,576]{1,0:T(8,128)(2,1)}) %reduce-scatter.23.cloned.1.call-update) | async-done | bytes 331792 | tf_op jit(solution)/shard_map/reduce_scatter | solution.py:294
  515.7 19.9 %reduce-scatter.17.cloned.1.call-done = bf16[288,576]{1,0:T(8,128)(2,1)} async-done(((bf16[576,576]{1,0:T(8,128)(2,1)}), bf16[288,576]{1,0:T(8,128)(2,1)}) %reduce-scatter.17.cloned.1.call-update) | async-done | bytes 331792 | tf_op jit(solution)/shard_map/reduce_scatter | solution.py:285
  535.6 14.2 %reduce-scatter.21.cloned.1.call-done = bf16[288,192]{1,0:T(8,128)(2,1)} async-done(((bf16[576,192]{1,0:T(8,128)(2,1)}), bf16[288,192]{1,0:T(8,128)(2,1)}) %reduce-scatter.21.cloned.1.call-update) | async-done | bytes 110608 | tf_op jit(solution)/shard_map/reduce_scatter | solution.py:291
  549.8 15.0 %reduce-scatter.19.cloned.1.call-done = bf16[288,192]{1,0:T(8,128)(2,1)} async-done(((bf16[576,192]{1,0:T(8,128)(2,1)}), bf16[288,192]{1,0:T(8,128)(2,1)}) %reduce-scatter.19.cloned.1.call-update) | async-done | bytes 110608 | tf_op jit(solution)/shard_map/reduce_scatter | solution.py:288
  564.8 4.9 all-reduce.7
  569.9 34.5 %all-reduce.4 = (bf16[288]{0:T(512)(128)(2,1)S(1)}, bf16[288]{0:T(512)(128)(2,1)S(1)}) all-reduce(bf16[288]{0:T(512)(128)(2,1)S(1)} %dynamic-slice.3, bf16[288]{0:T(512)(128)(2,1)S(1)} %dynamic-slice.5), channel_id=1, replica_groups=mesh['dp'=2,'context'=4,'tensor'=4] {'context','tensor'}, use_global_device_ids=true, to_apply=%region_14.15 | all-reduce | flops 576 | bytes 2304 | tf_op jit(solution)/shard_map/psum | solution.py:308
  605.6 14.5 %reduce-scatter.11.cloned.1.call-done = bf16[8,64,576]{2,1,0:T(8,128)(2,1)} async-done(((bf16[8,256,576]{2,1,0:T(8,128)(2,1)}), bf16[8,64,576]{2,1,0:T(8,128)(2,1)}) %reduce-scatter.11.cloned.1.call-update) | async-done | bytes 589840 | tf_op jit(solution)/shard_map/reduce_scatter | solution.py:168
  620.1 3.5 fusion.42
  623.6 93.3 %all-reduce.12.cloned.1.call-done = (bf16[288,576]{1,0:T(8,128)(2,1)}, bf16[288,192]{1,0:T(8,128)(2,1)}, bf16[288,192]{1,0:T(8,128)(2,1)}, bf16[288,576]{1,0:T(8,128)(2,1)}) async-done(((bf16[288,576]{1,0:T(8,128)(2,1)}, bf16[288,192]{1,0:T(8,128)(2,1)}, bf16[288,192]{1,0:T(8,128)(2,1)}, bf16[288,576]{1,0:T(8,128)(2,1)}), (bf16[288,576]{1,0:T(8,128)(2,1)}, bf16[288,192]{1,0:T(8,128)(2,1)}, ...) | async-done | bytes 884752 | tf_op jit(solution)/shard_map/psum | solution.py:310
  (262 shorter events, 98.2 us)
Async XLA Ops:
  7.2 23.8 %copy-start.8 = (bf16[8,64,576]{2,1,0:T(8,128)(2,1)S(1)}, bf16[8,64,576]{2,1,0:T(8,128)(2,1)}, u32[]{:S(2)}) copy-start(bf16[8,64,576]{2,1,0:T(8,128)(2,1)} %param.13) | copy-start | bytes 1769476
  7.2 89.8 %all-gather.4.cloned.1.call-start = ((), (), s32[]{:S(2)}) async-start(), calls=%async_computation.10 | async-start | bytes 6684672 | tf_op jit(solution)/shard_map/all_gather | solution.py:121
  16.9 14.8 %copy-start.34 = (f32[576]{0:T(1024)}, f32[576]{0:T(1024)S(1)}, u32[]{:S(2)}) copy-start(f32[576]{0:T(1024)S(1)} %convert_element_type.199) | copy-start | bytes 6916
  18.2 13.5 %copy-start.36 = (f32[8,64]{1,0:T(8,128)}, f32[8,64]{1,0:T(8,128)S(1)}, u32[]{:S(2)}) copy-start(f32[8,64]{1,0:T(8,128)S(1)} %add_rsqrt_fusion.1) | copy-start | bytes 6148
  31.2 11.1 %copy-start.10 = (bf16[8,64,576]{2,1,0:T(8,128)(2,1)}, bf16[8,64,576]{2,1,0:T(8,128)(2,1)S(1)}, u32[]{:S(2)}) copy-start(bf16[8,64,576]{2,1,0:T(8,128)(2,1)S(1)} %fusion.38) | copy-start | bytes 1769476
  32.2 1.6 copy-start.29
  33.7 163.3 %all-gather.6.cloned.1.call-start = ((), (), s32[]{:S(2)}) async-start(), calls=%async_computation.11 | async-start | bytes 3276800 | tf_op jit(solution)/shard_map/all_gather | solution.py:156
  45.8 2.0 copy-start.30
  138.1 3.2 copy-start.6
  141.3 2.9 copy-start.31
  141.4 11.2 %copy-start.32 = (bf16[288,384]{1,0:T(8,128)(2,1)S(1)}, bf16[288,384]{1,0:T(8,128)(2,1)}, u32[]{:S(2)}) copy-start(bf16[288,384]{1,0:T(8,128)(2,1)} %param.21) | copy-start | bytes 663556
  141.4 18.7 %copy-start.33 = (bf16[384,288]{0,1:T(8,128)(2,1)S(1)}, bf16[384,288]{0,1:T(8,128)(2,1)}, u32[]{:S(2)}) copy-start(bf16[384,288]{0,1:T(8,128)(2,1)} %param.22) | copy-start | bytes 663556
  143.4 108.7 %all-gather.8.cloned.1.call-start = ((), (), s32[]{:S(2)}) async-start(), calls=%async_computation.13 | async-start | bytes 3276800 | tf_op jit(solution)/shard_map/all_gather | solution.py:172
  144.2 171.6 %reduce-scatter.13.cloned.1.call-start = ((), (), s32[]{:S(2)}) async-start(), calls=%async_computation.14 | async-start | bytes 3276800 | tf_op jit(solution)/shard_map/reduce_scatter | solution.py:186
  197.0 3.6 copy-start.1
  197.0 3.6 copy-start.20
  252.2 6.8 copy-start.21
  259.0 1.6 copy-start.15
  259.0 1.6 copy-start.19
  264.6 1.7 copy-start.38
  264.6 111.0 %reduce-scatter.29.cloned.1.call-start = ((), (), s32[]{:S(2)}) async-start(), calls=%async_computation.22 | async-start | bytes 663552 | tf_op jit(solution)/shard_map/reduce_scatter | solution.py:303
  270.0 105.7 %reduce-scatter.25.cloned.1.call-start = ((), (), s32[]{:S(2)}) async-start(), calls=%async_computation.20 | async-start | bytes 663552 | tf_op jit(solution)/shard_map/reduce_scatter | solution.py:297
  292.5 83.2 %reduce-scatter.27.cloned.1.call-start = ((), (), s32[]{:S(2)}) async-start(), calls=%async_computation.21 | async-start | bytes 663552 | tf_op jit(solution)/shard_map/reduce_scatter | solution.py:300
  292.5 9.3 %copy-start.2 = (bf16[8,256,576]{2,1,0:T(8,128)(2,1)S(1)}, bf16[8,256,576]{2,1,0:T(8,128)(2,1)}, u32[]{:S(2)}) copy-start(bf16[8,256,576]{2,1,0:T(8,128)(2,1)} %all-gather.6.cloned.1.call-done) | copy-start | bytes 7077892
  292.6 9.3 %copy-start.16 = (bf16[2048,384]{1,0:T(8,128)(2,1)S(1)}, bf16[2048,384]{1,0:T(8,128)(2,1)}, u32[]{:S(2)}) copy-start(bf16[2048,384]{1,0:T(8,128)(2,1)} %copy-done.15) | copy-start | bytes 4718596
  304.0 156.3 %reduce-scatter.15.cloned.1.call-start = ((), (), s32[]{:S(2)}) async-start(), calls=%async_computation.15 | async-start | bytes 6684672 | tf_op jit(solution)/shard_map/reduce_scatter | solution.py:245
  315.8 2.2 copy-start.4
  315.8 2.2 copy-start.17
  315.8 4.6 copy-start.22
  321.9 6.5 copy-start.39
  324.8 3.7 copy-start.18
  344.6 11.9 %copy-start.7 = (bf16[8,64,3,3,64]{4,1,3,2,0:T(8,128)(2,1)S(1)}, bf16[8,64,3,3,64]{4,1,3,2,0:T(8,128)(2,1)}, u32[]{:S(2)}) copy-start(bf16[8,64,3,3,64]{4,1,3,2,0:T(8,128)(2,1)} %copy-done.6) | copy-start | bytes 1769476
  356.5 4.5 copy-start
  375.6 120.7 %all-reduce.14.cloned.1.call-start = ((), (), s32[]{:S(2)}) async-start(), calls=%async_computation.24 | async-start | bytes 1327104 | tf_op jit(solution)/shard_map/psum | solution.py:316
  376.3 139.4 %reduce-scatter.23.cloned.1.call-start = ((), (), s32[]{:S(2)}) async-start(), calls=%async_computation.19 | async-start | bytes 1105920 | tf_op jit(solution)/shard_map/reduce_scatter | solution.py:294
  379.9 155.7 %reduce-scatter.17.cloned.1.call-start = ((), (), s32[]{:S(2)}) async-start(), calls=%async_computation.16 | async-start | bytes 1105920 | tf_op jit(solution)/shard_map/reduce_scatter | solution.py:285
  390.1 159.7 %reduce-scatter.21.cloned.1.call-start = ((), (), s32[]{:S(2)}) async-start(), calls=%async_computation.18 | async-start | bytes 442368 | tf_op jit(solution)/shard_map/reduce_scatter | solution.py:291
  460.3 2.2 copy-start.27
  463.8 101.0 %reduce-scatter.19.cloned.1.call-start = ((), (), s32[]{:S(2)}) async-start(), calls=%async_computation.17 | async-start | bytes 442368 | tf_op jit(solution)/shard_map/reduce_scatter | solution.py:288
  465.7 154.4 %reduce-scatter.11.cloned.1.call-start = ((), (), s32[]{:S(2)}) async-start(), calls=%async_computation.12 | async-start | bytes 3276800 | tf_op jit(solution)/shard_map/reduce_scatter | solution.py:168
  471.2 30.2 %copy-start.14 = (bf16[576,576]{1,0:T(8,128)(2,1)S(1)}, bf16[576,576]{1,0:T(8,128)(2,1)}, u32[]{:S(2)}) copy-start(bf16[576,576]{1,0:T(8,128)(2,1)} %copy-done.13) | copy-start | bytes 1990660
  471.3 30.8 %copy-start.24 = (bf16[576,192]{1,0:T(8,128)(2,1)S(1)}, bf16[576,192]{1,0:T(8,128)(2,1)}, u32[]{:S(2)}) copy-start(bf16[576,192]{1,0:T(8,128)(2,1)} %copy-done.23) | copy-start | bytes 663556
  471.3 245.6 %all-reduce.12.cloned.1.call-start = ((), (), s32[]{:S(2)}) async-start(), calls=%async_computation.23 | async-start | bytes 2064384 | tf_op jit(solution)/shard_map/psum | solution.py:310
  499.7 3.7 copy-start.26
  503.4 3.1 copy-start.9
  503.4 3.1 copy-start.35
  503.4 3.1 copy-start.37
  506.4 113.6 %copy-start.5 = (f32[8,64,576]{2,1,0:T(8,128)S(1)}, f32[8,64,576]{2,1,0:T(8,128)}, u32[]{:S(2)}) copy-start(f32[8,64,576]{2,1,0:T(8,128)} %copy-done.3) | copy-start | bytes 3538948
  (7 other events, 7.8 us)
Sparse Core Ops, SparseCore 0:
  33.8 63.1 all-gather.3
  143.6 53.4 all-gather.5
  198.6 53.5 all-gather.7
  264.8 51.0 reduce-scatter.12
  318.5 13.2 reduce-scatter.28
  334.5 13.6 reduce-scatter.24
  351.1 13.7 reduce-scatter.26
  375.7 84.6 reduce-scatter.14
  462.9 33.2 all-reduce.13
  498.3 17.3 reduce-scatter.22
  518.6 16.9 reduce-scatter.16
  537.7 12.0 reduce-scatter.20
  552.6 12.1 reduce-scatter.18
  566.9 53.1 reduce-scatter.10
  623.8 93.1 all-reduce.11
where the time goes:
time: 739 us; the launch traced here: 731 us
  waiting for transfers between devices  392 us (53%)
  matrix products  99.6 us (13%)
  blocking collectives  96.6 us (13%)
  local copies, waits for them, and re-layouts  71.4 us (10%)
  other arithmetic  53.2 us (7%)
  between operations  16.3 us (2%)
    psum x1, waiting for transfers between devices, body(): lax.psum(shards[2].astype(jnp.bfloat16), ('context', 'tensor'))  93.3 us
    reduce_scatter x1, waiting for transfers between devices, body(): lax.psum_scatter(grad_kv.astype(jnp.bfloat16), ('context', 'tensor'), sca...  70.2 us
    all_gather x1, waiting for transfers between devices, body(): lax.all_gather(out_grad, 'tensor', axis=1, tiled=True)  48.1 us
    all_gather x1, waiting for transfers between devices, body(): lax.all_gather(kv_local, ('context', 'tensor'), axis=1, tiled=True)  40.9 us
    psum x1, blocking collectives, body(): lax.psum(shards[0].astype(jnp.bfloat16), ('context', 'tensor'))  34.5 us
    all_gather x1, waiting for transfers between devices, body(): ffn_rows = lax.all_gather(ffn_low, 'tensor', axis=1, tiled=True)  30.1 us
    psum x1, waiting for transfers between devices, body(): lax.psum(shards[6].astype(jnp.bfloat16), 'context').astype(jnp.float32)  24.2 us
    reduce_scatter x1, waiting for transfers between devices, body(): lax.psum_scatter(query_grad.astype(jnp.bfloat16), 'dp', scatter_dimension...  19.9 us
  transfers between devices with their start and end apart: 15, of which 12 were waited for; matrix products, arithmetic and copies ran while one was open for 20% of the time, Pallas kernels for 0%

commit v1 on v0

--- a/solution.py
+++ b/solution.py
@@ -1,13 +1,41 @@
+import functools
 import jax
 import jax.numpy as jnp
 from jax import lax
 from jax.sharding import PartitionSpec as P
+from jax.lax import axis_index, axis_size, ppermute
 
 HEADS = 9
 KV_HEADS = 3
 HEAD_DIM = 64
 EPS = 1e-05
 ROPE_BASE = 100000.0
+
+
+def keep_up_the_sizes(in_array, comm_axis):
+    field_out = axis_index(comm_axis)
+    b_next = axis_size(comm_axis)
+    z, local_next, value_now = (b_next, field_out, in_array.shape[1])
+    made = [j * z if t == 1 else j for t, j in enumerate(in_array.shape)]
+    main = lax.dynamic_update_slice_in_dim(
+        jnp.zeros(made, in_array.dtype), in_array, local_next * value_now, axis=1
+    )
+    u_next = far_arr = in_array
+    for dev_i in range(1, z // 2 + 1):
+        heard = list(map(lambda t: (t, (t + 1) % z), range(z)))
+        u_next = ppermute(u_next, comm_axis, heard)
+        main = lax.dynamic_update_slice_in_dim(
+            main, u_next, (local_next - dev_i) % z * value_now, axis=1
+        )
+        if 2 * dev_i < z:
+            far_arr = ppermute(far_arr, comm_axis, list(map(lambda t: (t, (t - 1) % z), range(z))))
+            main = lax.dynamic_update_slice_in_dim(
+                main, far_arr, (local_next + dev_i) % z * value_now, axis=1
+            )
+    return main
+
+
+see_ratios = functools.partial(keep_up_the_sizes, comm_axis=("context", "tensor"))
 
 
 def rotary(places, half_dim):
@@ -118,7 +146,7 @@
         .reshape(seq_count, local_len, kv_width)
     )
     kv_local = jnp.concatenate([keys_low, value_rows.astype(jnp.bfloat16)], axis=-1)
-    kv_whole = lax.all_gather(kv_local, ("context", "tensor"), axis=1, tiled=True)
+    kv_whole = see_ratios(kv_local)
     seq_len = kv_whole.shape[1]
     query_groups = queries_low.reshape(seq_count, local_len, KV_HEADS, repeat, HEAD_DIM)
 

time: 739 us -> 999 us (1.35)
  local copies, waits for them, and re-layouts: 71.4 us -> 202 us
  starting transfers between devices: 1 us -> 72.7 us
  waiting for transfers between devices: 392 us -> 441 us
    dynamic_update_slice x0 -> x16, local copies, waits for them, and re-layouts: none -> 107 us  [the longest x8 52.7 us: keep_up_the_sizes(): lax.dynamic_update_slice_in_dim(main, u_next, (local_next - dev_i) % z *...]
    ppermute x0 -> x15, starting transfers between devices: none -> 71.9 us  [the longest x8 55.9 us: keep_up_the_sizes(): u_next = ppermute(u_next, comm_axis, heard)]
    ppermute x0 -> x15, waiting for transfers between devices: none -> 40.3 us  [the longest x8 39.4 us: keep_up_the_sizes(): u_next = ppermute(u_next, comm_axis, heard)]
    reduce_scatter x1, waiting for transfers between devices: 11.7 us -> 46.5 us  [body(): lax.psum_scatter(grad_ffn_part.astype(jnp.bfloat16), 'tensor', scatter_di...]
    psum x1, waiting for transfers between devices: 93.3 us -> 70.6 us  [body(): lax.psum(shards[2].astype(jnp.bfloat16), ('context', 'tensor'))]
    ppermute x0 -> x15, local copies, waits for them, and re-layouts: none -> 20.8 us  [the longest x8 11.2 us: keep_up_the_sizes(): u_next = ppermute(u_next, comm_axis, heard)]
    dynamic_slice x16 -> x0, local copies, waits for them, and re-layouts: 12.1 us -> none  [body(): attended, log_sums = lax.map(attend_one, (query_groups, kv_whole))]
    all_gather x1, waiting for transfers between devices: 40.9 us -> 29.9 us  [body(): piece = lax.all_gather(kv_local, ('context', 'tensor'), axis=1, tiled=True)]
  transfers between devices with their start and end apart: 15 -> 30, of which waited for: 12 -> 20; matrix products, arithmetic and copies ran while one was open for 20% -> 28% of each run, Pallas kernels for 0% -> 0%
where the time goes in v1:
time: 999 us; the launch traced here: 988 us
  waiting for transfers between devices  441 us (44%)
  local copies, waits for them, and re-layouts  202 us (20%)
  matrix products  105 us (11%)
  blocking collectives  97.3 us (10%)
  starting transfers between devices  72.7 us (7%)
  other arithmetic  51.5 us (5%)
  between operations  18.2 us (2%)
    psum x1, waiting for transfers between devices, body(): lax.psum(shards[2].astype(jnp.bfloat16), ('context', 'tensor'))  70.6 us
    reduce_scatter x1, waiting for transfers between devices, body(): lax.psum_scatter(grad_kv.astype(jnp.bfloat16), ('context', 'tensor'), sca...  69.3 us
    ppermute x8, starting transfers between devices, keep_up_the_sizes(): u_next = ppermute(u_next, comm_axis, heard)  55.9 us
    dynamic_update_slice x8, local copies, waits for them, and re-layouts, keep_up_the_sizes(): lax.dynamic_update_slice_in_dim(main, u_next, (local_next - dev_i) % z *...  52.7 us
    dynamic_update_slice x7, local copies, waits for them, and re-layouts, keep_up_the_sizes(): lax.dynamic_update_slice_in_dim(main, far_arr, (local_next + dev_i) % z *...  48.3 us
    all_gather x1, waiting for transfers between devices, body(): lax.all_gather(out_grad, 'tensor', axis=1, tiled=True)  46.6 us
    reduce_scatter x1, waiting for transfers between devices, body(): lax.psum_scatter(grad_ffn_part.astype(jnp.bfloat16), 'tensor', scatter_di...  46.5 us
    ppermute x8, waiting for transfers between devices, keep_up_the_sizes(): u_next = ppermute(u_next, comm_axis, heard)  39.4 us
  transfers between devices with their start and end apart: 30, of which 20 were waited for; matrix products, arithmetic and copies ran while one was open for 28% of the time, Pallas kernels for 0%

profile of v1, /device:TPU:0, one launch (start us, length us, event | category | flops | bytes accessed | tf_op | source)
XLA Modules:
  0.0 987.8 jit_solution(1084754415344416647)
XLA Ops:
  38.2 8.9 collective-permute-done
  47.1 6.4 collective-permute-start.2
  56.3 7.8 collective-permute-done.2
  64.0 9.6 collective-permute-start.4
  74.7 6.4 collective-permute-done.4
  81.1 10.1 %collective-permute-start.6 = (bf16[8,64,384]{2,1,0:T(8,128)(2,1)S(1)}, bf16[8,64,384]{2,1,0:T(8,128)(2,1)S(1)}, u32[]{:S(2)}, u32[]{:S(2)}) collective-permute-start(bf16[8,64,384]{2,1,0:T(8,128)(2,1)S(1)} %collective-permute-done.4), channel_id=1, source_target_pairs={{0,1},{1,2},{2,3},{3,4},{4,5},{5,6},{6,7},{7,8},{8,9},{9,10},{10,1... | collective-permute-start | bytes 1179656 | tf_op jit(solution)/shard_map/ppermute | solution.py:26
  93.8 6.6 collective-permute-done.6
  100.5 7.5 collective-permute-start.8
  116.2 9.8 collective-permute-start.10
  129.3 6.3 collective-permute-done.10
  135.5 7.8 collective-permute-start.12
  143.3 9.0 all_gather.39
  173.4 10.9 %all_gather.40 = bf16[576,576]{1,0:T(8,128)(2,1)S(1)} all-gather(bf16[288,576]{1,0:T(8,128)(2,1)S(1)} %copy-done.41), channel_id=1, replica_groups=mesh['dp'=2,'context'=4,'tensor'=4] {'dp'}, dimensions={0}, use_global_device_ids=true | all-gather | bytes 995328 | tf_op jit(solution)/shard_map/all_gather | solution.py:116
  185.9 6.9 dynamic_update_slice.57
  194.2 7.5 dynamic_update_slice.58
  217.3 7.4 dynamic_update_slice.61
  226.0 7.4 dynamic_update_slice.62
  249.7 7.4 dynamic_update_slice.65
  258.5 7.4 dynamic_update_slice.66
  282.1 7.4 dynamic_update_slice.69
  290.9 7.8 dynamic_update_slice.70
  306.2 38.5 %while.13 = (s32[]{:T(128)}, f32[8,64,576]{1,2,0:T(8,128)}, f32[8,3,3,64]{3,2,1,0:T(4,128)}, bf16[8,1024,384]{1,2,0:T(8,128)(2,1)}, bf16[8,64,3,3,64]{4,1,3,2,0:T(8,128)(2,1)S(1)}, /*index=5*/s32[]{:T(128)}, s32[]{:T(128)}) while((s32[]{:T(128)}, f32[8,64,576]{1,2,0:T(8,128)}, f32[8,3,3,64]{3,2,1,0:T(4,128)}, ...), condition=%wide.region_4.5_spmd.clone, body=%wide.region_1.4_spmd.clone.sunk | while | flops 158137856 | bytes 12032361 | solution.py:175
  350.6 7.0 all_gather.43
  357.6 6.6 all_gather.44
  364.2 6.7 all_gather.45
  370.9 36.8 %all-gather.4.cloned.1.call-done = bf16[8,256,576]{2,1,0:T(8,128)(2,1)} async-done(((bf16[8,64,576]{2,1,0:T(8,128)(2,1)}), bf16[8,256,576]{2,1,0:T(8,128)(2,1)}) %all-gather.4.cloned.1.call-update) | async-done | bytes 2359312 | tf_op jit(solution)/shard_map/all_gather | solution.py:184
  416.2 46.6 %all-gather.6.cloned.1.call-done = bf16[8,256,576]{2,1,0:T(8,128)(2,1)} async-done(((bf16[8,64,576]{2,1,0:T(8,128)(2,1)}), bf16[8,256,576]{2,1,0:T(8,128)(2,1)}) %all-gather.6.cloned.1.call-update) | async-done | bytes 2359312 | tf_op jit(solution)/shard_map/all_gather | solution.py:200
  462.8 7.7 multiply_convert_fusion
  492.9 46.5 %reduce-scatter.13.cloned.1.call-done = bf16[8,64,576]{2,1,0:T(8,128)(2,1)} async-done(((bf16[8,256,576]{2,1,0:T(8,128)(2,1)}), bf16[8,64,576]{2,1,0:T(8,128)(2,1)}) %reduce-scatter.13.cloned.1.call-update) | async-done | bytes 589840 | tf_op jit(solution)/shard_map/reduce_scatter | solution.py:214
  549.2 29.9 %all-gather.8.cloned.1.call-done = bf16[8,1024,384]{2,1,0:T(8,128)(2,1)} async-done(((bf16[8,64,384]{2,1,0:T(8,128)(2,1)}), bf16[8,1024,384]{2,1,0:T(8,128)(2,1)}) %all-gather.8.cloned.1.call-update) | async-done | bytes 6291472 | tf_op jit(solution)/shard_map/all_gather | solution.py:232
  579.0 6.7 fusion.62
  585.7 6.3 copy.120
  597.0 9.2 fusion.67
  606.2 10.0 %bitcast_convert_fusion = bf16[8,3,64,1024]{3,2,1,0:T(8,128)(2,1)} fusion(f32[8,3,1024,64,3]{2,3,4,1,0:T(8,128)} %fusion.67, f32[8,3,3,64]{3,2,1,0:T(4,128)S(1)} %copy-done.58, pred[64,1024]{1,0:T(8,128)(4,1)S(1)} %copy-done.53, bf16[8,64,3,3,64]{1,0,4,3,2:T(8,128)(2,1)S(1)} %copy-done.19), kind=kOutput, calls=%fused_computation.31 | convolution fusion | flops 624427008 | bytes 22693888 | tf_op jit(solution)/shard_map/sgrqk,sqgre->skge/dot_general | solution.py:258
  616.2 6.2 copy.128
  622.4 12.0 %fusion.12 = bf16[8,3,3,64,1024]{4,3,2,1,0:T(8,128)(2,1)S(1)} fusion(f32[8,3,1024,64,3]{2,3,4,1,0:T(8,128)} %fusion.67, f32[8,3,3,64]{3,2,1,0:T(4,128)S(1)} %copy-done.54, f32[8,3,3,64]{3,2,1,0:T(4,128)S(1)} %copy-done.58, pred[64,1024]{1,0:T(8,128)(4,1)S(1)} %copy-done.53, bf16[8,1024,3,64,1]{1,3,4,2,0:T(8,128)(2,1)} %bitcast.218, ...), kind=kOutput, calls=%fused_computation.20 | convolution fusion | flops 632291328 | bytes 32149504 | tf_op jit(solution)/shard_map/sqgre,skge->sgrqk/dot_general | solution.py:242
  638.9 6.1 copy.127
  645.1 8.3 pad_maximum_fusion
  657.6 6.3 convolution_multiply_fusion
  667.9 69.3 %reduce-scatter.15.cloned.1.call-done = bf16[8,64,384]{2,1,0:T(8,128)(2,1)} async-done(((bf16[8,1024,384]{2,1,0:T(8,128)(2,1)}), bf16[8,64,384]{2,1,0:T(8,128)(2,1)}) %reduce-scatter.15.cloned.1.call-update) | async-done | bytes 393232 | tf_op jit(solution)/shard_map/reduce_scatter | solution.py:273
  749.2 23.8 %all-reduce.14.cloned.1.call-done = (bf16[288,384]{1,0:T(8,128)(2,1)}, bf16[288,384]{1,0:T(8,128)(2,1)}, bf16[384,288]{0,1:T(8,128)(2,1)}) async-done(((bf16[288,384]{1,0:T(8,128)(2,1)}, bf16[288,384]{1,0:T(8,128)(2,1)}, bf16[384,288]{0,1:T(8,128)(2,1)}), (bf16[288,384]{1,0:T(8,128)(2,1)}, bf16[288,384]{1,0:T(8,128)(2,1)}, bf16[384,288]{0,1:T(8,128)(2,1)})) %all-reduce.14.cloned.1.call-update) | async-done | bytes 663568 | tf_op jit(solution)/shard_map/psum | solution.py:344
  783.8 8.9 reduce-scatter.23.cloned.1.call-done
  792.7 19.7 %reduce-scatter.17.cloned.1.call-done = bf16[288,576]{1,0:T(8,128)(2,1)} async-done(((bf16[576,576]{1,0:T(8,128)(2,1)}), bf16[288,576]{1,0:T(8,128)(2,1)}) %reduce-scatter.17.cloned.1.call-update) | async-done | bytes 331792 | tf_op jit(solution)/shard_map/reduce_scatter | solution.py:313
  812.4 14.4 %reduce-scatter.21.cloned.1.call-done = bf16[288,192]{1,0:T(8,128)(2,1)} async-done(((bf16[576,192]{1,0:T(8,128)(2,1)}), bf16[288,192]{1,0:T(8,128)(2,1)}) %reduce-scatter.21.cloned.1.call-update) | async-done | bytes 110608 | tf_op jit(solution)/shard_map/reduce_scatter | solution.py:319
  826.8 14.8 %reduce-scatter.19.cloned.1.call-done = bf16[288,192]{1,0:T(8,128)(2,1)} async-done(((bf16[576,192]{1,0:T(8,128)(2,1)}), bf16[288,192]{1,0:T(8,128)(2,1)}) %reduce-scatter.19.cloned.1.call-update) | async-done | bytes 110608 | tf_op jit(solution)/shard_map/reduce_scatter | solution.py:316
  846.7 34.2 %all-reduce.4 = (bf16[288]{0:T(512)(128)(2,1)S(1)}, bf16[288]{0:T(512)(128)(2,1)S(1)}) all-reduce(bf16[288]{0:T(512)(128)(2,1)S(1)} %dynamic-slice.3, bf16[288]{0:T(512)(128)(2,1)S(1)} %dynamic-slice.5), channel_id=1, replica_groups=mesh['dp'=2,'context'=4,'tensor'=4] {'context','tensor'}, use_global_device_ids=true, to_apply=%region_14.15 | all-reduce | flops 576 | bytes 2304 | tf_op jit(solution)/shard_map/psum | solution.py:336
  882.1 16.9 %reduce-scatter.11.cloned.1.call-done = bf16[8,64,576]{2,1,0:T(8,128)(2,1)} async-done(((bf16[8,256,576]{2,1,0:T(8,128)(2,1)}), bf16[8,64,576]{2,1,0:T(8,128)(2,1)}) %reduce-scatter.11.cloned.1.call-update) | async-done | bytes 589840 | tf_op jit(solution)/shard_map/reduce_scatter | solution.py:196
  902.6 70.6 %all-reduce.12.cloned.1.call-done = (bf16[288,576]{1,0:T(8,128)(2,1)}, bf16[288,192]{1,0:T(8,128)(2,1)}, bf16[288,192]{1,0:T(8,128)(2,1)}, bf16[288,576]{1,0:T(8,128)(2,1)}) async-done(((bf16[288,576]{1,0:T(8,128)(2,1)}, bf16[288,192]{1,0:T(8,128)(2,1)}, bf16[288,192]{1,0:T(8,128)(2,1)}, bf16[288,576]{1,0:T(8,128)(2,1)}), (bf16[288,576]{1,0:T(8,128)(2,1)}, bf16[288,192]{1,0:T(8,128)(2,1)}, ...) | async-done | bytes 884752 | tf_op jit(solution)/shard_map/psum | solution.py:338
  (355 shorter events, 271.5 us)
Async XLA Ops:
  8.0 399.7 %all-gather.4.cloned.1.call-start = ((), (), s32[]{:S(2)}) async-start(), calls=%async_computation.10 | async-start | bytes 3276800 | tf_op jit(solution)/shard_map/all_gather | solution.py:184
  32.1 120.7 %copy-start.9 = (bf16[8,64,576]{2,1,0:T(8,128)(2,1)}, bf16[8,64,576]{2,1,0:T(8,128)(2,1)S(1)}, u32[]{:S(2)}) copy-start(bf16[8,64,576]{2,1,0:T(8,128)(2,1)S(1)} %fusion.38) | copy-start | bytes 1769476
  33.1 123.5 %copy-start.30 = (f32[64,32]{0,1:T(8,128)}, f32[64,32]{0,1:T(8,128)S(1)}, u32[]{:S(2)}) copy-start(f32[64,32]{0,1:T(8,128)S(1)} %get-tuple-element.112) | copy-start | bytes 24580
  33.7 124.0 %copy-start.20 = (bf16[8,64,384]{2,1,0:T(8,128)(2,1)}, bf16[8,64,384]{2,1,0:T(8,128)(2,1)S(1)}, u32[]{:S(2)}) copy-start(bf16[8,64,384]{2,1,0:T(8,128)(2,1)S(1)} %pad_maximum_fusion.3) | copy-start | bytes 1179652
  33.7 13.4 %collective-permute-start = (bf16[8,64,384]{2,1,0:T(8,128)(2,1)S(1)}, bf16[8,64,384]{2,1,0:T(8,128)(2,1)S(1)}, u32[]{:S(2)}, u32[]{:S(2)}) collective-permute-start(bf16[8,64,384]{2,1,0:T(8,128)(2,1)S(1)} %pad_maximum_fusion.3), channel_id=1, source_target_pairs={{0,1},{1,2},{2,3},{3,4},{4,5},{5,6},{6,7},{7,8},{8,9},{9,10},{10,1... | collective-permute-start | bytes 1179656 | tf_op jit(solution)/shard_map/ppermute | solution.py:26
  35.8 18.4 %collective-permute-start.1 = (bf16[8,64,384]{2,1,0:T(8,128)(2,1)S(1)}, bf16[8,64,384]{2,1,0:T(8,128)(2,1)S(1)}, u32[]{:S(2)}, u32[]{:S(2)}) collective-permute-start(bf16[8,64,384]{2,1,0:T(8,128)(2,1)S(1)} %pad_maximum_fusion.3), channel_id=1, source_target_pairs={{0,15},{1,0},{2,1},{3,2},{4,3},{5,4},{6,5},{7,6},{8,7},{9,8},{10,9... | collective-permute-start | bytes 1179656 | tf_op jit(solution)/shard_map/ppermute | solution.py:31
  47.1 105.2 %copy-start.34 = (bf16[8,64,384]{2,1,0:T(8,128)(2,1)}, bf16[8,64,384]{2,1,0:T(8,128)(2,1)S(1)}, u32[]{:S(2)}) copy-start(bf16[8,64,384]{2,1,0:T(8,128)(2,1)S(1)} %collective-permute-done) | copy-start | bytes 1179652
  47.1 16.9 %collective-permute-start.2 = (bf16[8,64,384]{2,1,0:T(8,128)(2,1)S(1)}, bf16[8,64,384]{2,1,0:T(8,128)(2,1)S(1)}, u32[]{:S(2)}, u32[]{:S(2)}) collective-permute-start(bf16[8,64,384]{2,1,0:T(8,128)(2,1)S(1)} %collective-permute-done), channel_id=1, source_target_pairs={{0,1},{1,2},{2,3},{3,4},{4,5},{5,6},{6,7},{7,8},{8,9},{9,10},{10,1... | collective-permute-start | bytes 1179656 | tf_op jit(solution)/shard_map/ppermute | solution.py:26
  54.2 81.3 %copy-start.32 = (bf16[8,64,384]{2,1,0:T(8,128)(2,1)}, bf16[8,64,384]{2,1,0:T(8,128)(2,1)S(1)}, u32[]{:S(2)}) copy-start(bf16[8,64,384]{2,1,0:T(8,128)(2,1)S(1)} %collective-permute-done.1) | copy-start | bytes 1179652
  54.2 19.4 %collective-permute-start.3 = (bf16[8,64,384]{2,1,0:T(8,128)(2,1)S(1)}, bf16[8,64,384]{2,1,0:T(8,128)(2,1)S(1)}, u32[]{:S(2)}, u32[]{:S(2)}) collective-permute-start(bf16[8,64,384]{2,1,0:T(8,128)(2,1)S(1)} %collective-permute-done.1), channel_id=1, source_target_pairs={{0,15},{1,0},{2,1},{3,2},{4,3},{5,4},{6,5},{7,6},{8,7},{9,8},{10,9... | collective-permute-start | bytes 1179656 | tf_op jit(solution)/shard_map/ppermute | solution.py:31
  64.0 71.5 %copy-start.33 = (bf16[8,64,384]{2,1,0:T(8,128)(2,1)}, bf16[8,64,384]{2,1,0:T(8,128)(2,1)S(1)}, u32[]{:S(2)}) copy-start(bf16[8,64,384]{2,1,0:T(8,128)(2,1)S(1)} %collective-permute-done.2) | copy-start | bytes 1179652
  64.0 17.1 %collective-permute-start.4 = (bf16[8,64,384]{2,1,0:T(8,128)(2,1)S(1)}, bf16[8,64,384]{2,1,0:T(8,128)(2,1)S(1)}, u32[]{:S(2)}, u32[]{:S(2)}) collective-permute-start(bf16[8,64,384]{2,1,0:T(8,128)(2,1)S(1)} %collective-permute-done.2), channel_id=1, source_target_pairs={{0,1},{1,2},{2,3},{3,4},{4,5},{5,6},{6,7},{7,8},{8,9},{9,10},{10,1... | collective-permute-start | bytes 1179656 | tf_op jit(solution)/shard_map/ppermute | solution.py:26
  73.6 78.7 %copy-start.35 = (bf16[8,64,384]{2,1,0:T(8,128)(2,1)}, bf16[8,64,384]{2,1,0:T(8,128)(2,1)S(1)}, u32[]{:S(2)}) copy-start(bf16[8,64,384]{2,1,0:T(8,128)(2,1)S(1)} %collective-permute-done.3) | copy-start | bytes 1179652
  73.6 17.6 %collective-permute-start.5 = (bf16[8,64,384]{2,1,0:T(8,128)(2,1)S(1)}, bf16[8,64,384]{2,1,0:T(8,128)(2,1)S(1)}, u32[]{:S(2)}, u32[]{:S(2)}) collective-permute-start(bf16[8,64,384]{2,1,0:T(8,128)(2,1)S(1)} %collective-permute-done.3), channel_id=1, source_target_pairs={{0,15},{1,0},{2,1},{3,2},{4,3},{5,4},{6,5},{7,6},{8,7},{9,8},{10,9... | collective-permute-start | bytes 1179656 | tf_op jit(solution)/shard_map/ppermute | solution.py:31
  81.1 71.3 %copy-start.36 = (bf16[8,64,384]{2,1,0:T(8,128)(2,1)}, bf16[8,64,384]{2,1,0:T(8,128)(2,1)S(1)}, u32[]{:S(2)}) copy-start(bf16[8,64,384]{2,1,0:T(8,128)(2,1)S(1)} %collective-permute-done.4) | copy-start | bytes 1179652
  81.1 19.4 %collective-permute-start.6 = (bf16[8,64,384]{2,1,0:T(8,128)(2,1)S(1)}, bf16[8,64,384]{2,1,0:T(8,128)(2,1)S(1)}, u32[]{:S(2)}, u32[]{:S(2)}) collective-permute-start(bf16[8,64,384]{2,1,0:T(8,128)(2,1)S(1)} %collective-permute-done.4), channel_id=1, source_target_pairs={{0,1},{1,2},{2,3},{3,4},{4,5},{5,6},{6,7},{7,8},{8,9},{9,10},{10,1... | collective-permute-start | bytes 1179656 | tf_op jit(solution)/shard_map/ppermute | solution.py:26
  91.2 61.2 %copy-start.37 = (bf16[8,64,384]{2,1,0:T(8,128)(2,1)}, bf16[8,64,384]{2,1,0:T(8,128)(2,1)S(1)}, u32[]{:S(2)}) copy-start(bf16[8,64,384]{2,1,0:T(8,128)(2,1)S(1)} %collective-permute-done.5) | copy-start | bytes 1179652
  91.2 17.0 %collective-permute-start.7 = (bf16[8,64,384]{2,1,0:T(8,128)(2,1)S(1)}, bf16[8,64,384]{2,1,0:T(8,128)(2,1)S(1)}, u32[]{:S(2)}, u32[]{:S(2)}) collective-permute-start(bf16[8,64,384]{2,1,0:T(8,128)(2,1)S(1)} %collective-permute-done.5), channel_id=1, source_target_pairs={{0,15},{1,0},{2,1},{3,2},{4,3},{5,4},{6,5},{7,6},{8,7},{9,8},{10,9... | collective-permute-start | bytes 1179656 | tf_op jit(solution)/shard_map/ppermute | solution.py:31
  100.5 15.7 %collective-permute-start.8 = (bf16[8,64,384]{2,1,0:T(8,128)(2,1)S(1)}, bf16[8,64,384]{2,1,0:T(8,128)(2,1)S(1)}, u32[]{:S(2)}, u32[]{:S(2)}) collective-permute-start(bf16[8,64,384]{2,1,0:T(8,128)(2,1)S(1)} %collective-permute-done.6), channel_id=1, source_target_pairs={{0,1},{1,2},{2,3},{3,4},{4,5},{5,6},{6,7},{7,8},{8,9},{9,10},{10,1... | collective-permute-start | bytes 1179656 | tf_op jit(solution)/shard_map/ppermute | solution.py:26
  108.2 17.8 %collective-permute-start.9 = (bf16[8,64,384]{2,1,0:T(8,128)(2,1)S(1)}, bf16[8,64,384]{2,1,0:T(8,128)(2,1)}, u32[]{:S(2)}, u32[]{:S(2)}) collective-permute-start(bf16[8,64,384]{2,1,0:T(8,128)(2,1)S(1)} %collective-permute-done.7), channel_id=1, source_target_pairs={{0,15},{1,0},{2,1},{3,2},{4,3},{5,4},{6,5},{7,6},{8,7},{9,8},{10,9... | collective-permute-start | bytes 1179656 | tf_op jit(solution)/shard_map/ppermute | solution.py:31
  116.2 19.3 %collective-permute-start.10 = (bf16[8,64,384]{2,1,0:T(8,128)(2,1)S(1)}, bf16[8,64,384]{2,1,0:T(8,128)(2,1)}, u32[]{:S(2)}, u32[]{:S(2)}) collective-permute-start(bf16[8,64,384]{2,1,0:T(8,128)(2,1)S(1)} %collective-permute-done.8), channel_id=1, source_target_pairs={{0,1},{1,2},{2,3},{3,4},{4,5},{5,6},{6,7},{7,8},{8,9},{9,10},{10,1... | collective-permute-start | bytes 1179656 | tf_op jit(solution)/shard_map/ppermute | solution.py:26
  126.0 27.8 %collective-permute-start.11 = (bf16[8,64,384]{2,1,0:T(8,128)(2,1)}, bf16[8,64,384]{2,1,0:T(8,128)(2,1)}, u32[]{:S(2)}, u32[]{:S(2)}) collective-permute-start(bf16[8,64,384]{2,1,0:T(8,128)(2,1)} %collective-permute-done.9), channel_id=1, source_target_pairs={{0,15},{1,0},{2,1},{3,2},{4,3},{5,4},{6,5},{7,6},{8,7},{9,8},{10,9... | collective-permute-start | bytes 1179656 | tf_op jit(solution)/shard_map/ppermute | solution.py:31
  135.5 18.4 %collective-permute-start.12 = (bf16[8,64,384]{2,1,0:T(8,128)(2,1)}, bf16[8,64,384]{2,1,0:T(8,128)(2,1)}, u32[]{:S(2)}, u32[]{:S(2)}) collective-permute-start(bf16[8,64,384]{2,1,0:T(8,128)(2,1)} %collective-permute-done.10), channel_id=1, source_target_pairs={{0,1},{1,2},{2,3},{3,4},{4,5},{5,6},{6,7},{7,8},{8,9},{9,10},{10,1... | collective-permute-start | bytes 1179656 | tf_op jit(solution)/shard_map/ppermute | solution.py:26
  153.9 135.7 %collective-permute-start.13 = (bf16[8,64,384]{2,1,0:T(8,128)(2,1)}, bf16[8,64,384]{2,1,0:T(8,128)(2,1)}, u32[]{:S(2)}, u32[]{:S(2)}) collective-permute-start(bf16[8,64,384]{2,1,0:T(8,128)(2,1)} %collective-permute-done.11), channel_id=1, source_target_pairs={{0,15},{1,0},{2,1},{3,2},{4,3},{5,4},{6,5},{7,6},{8,7},{9,8},{10,9... | collective-permute-start | bytes 1179656 | tf_op jit(solution)/shard_map/ppermute | solution.py:31
  154.0 144.8 %collective-permute-start.14 = (bf16[8,64,384]{2,1,0:T(8,128)(2,1)}, bf16[8,64,384]{2,1,0:T(8,128)(2,1)}, u32[]{:S(2)}, u32[]{:S(2)}) collective-permute-start(bf16[8,64,384]{2,1,0:T(8,128)(2,1)} %collective-permute-done.12), channel_id=1, source_target_pairs={{0,1},{1,2},{2,3},{3,4},{4,5},{5,6},{6,7},{7,8},{8,9},{9,10},{10,1... | collective-permute-start | bytes 1179656 | tf_op jit(solution)/shard_map/ppermute | solution.py:26
  158.9 383.3 %copy-start.45 = (f32[576]{0:T(1024)}, f32[576]{0:T(1024)S(1)}, u32[]{:S(2)}) copy-start(f32[576]{0:T(1024)S(1)} %convert_element_type.206) | copy-start | bytes 6916
  184.3 160.4 %copy-start.22 = (bf16[576,576]{1,0:T(8,128)(2,1)}, bf16[576,576]{1,0:T(8,128)(2,1)S(1)}, u32[]{:S(2)}) copy-start(bf16[576,576]{1,0:T(8,128)(2,1)S(1)} %all_gather.40) | copy-start | bytes 1990660
  347.8 194.5 %copy-start.47 = (f32[8,64]{1,0:T(8,128)}, f32[8,64]{1,0:T(8,128)S(1)}, u32[]{:S(2)}) copy-start(f32[8,64]{1,0:T(8,128)S(1)} %add_rsqrt_fusion) | copy-start | bytes 6148
  349.8 113.0 %all-gather.6.cloned.1.call-start = ((), (), s32[]{:S(2)}) async-start(), calls=%async_computation.12 | async-start | bytes 3276800 | tf_op jit(solution)/shard_map/all_gather | solution.py:200
  350.6 188.9 %reduce-scatter.13.cloned.1.call-start = ((), (), s32[]{:S(2)}) async-start(), calls=%async_computation.13 | async-start | bytes 3276800 | tf_op jit(solution)/shard_map/reduce_scatter | solution.py:214
  479.4 99.7 %all-gather.8.cloned.1.call-start = ((), (), s32[]{:S(2)}) async-start(), calls=%async_computation.14 | async-start | bytes 6684672 | tf_op jit(solution)/shard_map/all_gather | solution.py:232
  480.0 173.5 %reduce-scatter.29.cloned.1.call-start = ((), (), s32[]{:S(2)}) async-start(), calls=%async_computation.22 | async-start | bytes 663552 | tf_op jit(solution)/shard_map/reduce_scatter | solution.py:331
  484.4 169.0 %reduce-scatter.25.cloned.1.call-start = ((), (), s32[]{:S(2)}) async-start(), calls=%async_computation.20 | async-start | bytes 663552 | tf_op jit(solution)/shard_map/reduce_scatter | solution.py:325
  488.1 165.4 %reduce-scatter.27.cloned.1.call-start = ((), (), s32[]{:S(2)}) async-start(), calls=%async_computation.21 | async-start | bytes 663552 | tf_op jit(solution)/shard_map/reduce_scatter | solution.py:328
  489.1 53.1 %copy-start.17 = (bf16[8,64,576]{2,1,0:T(8,128)(2,1)S(1)}, bf16[8,64,576]{2,1,0:T(8,128)(2,1)}, u32[]{:S(2)}) copy-start(bf16[8,64,576]{2,1,0:T(8,128)(2,1)} %param.23) | copy-start | bytes 1769476
  492.9 244.3 %reduce-scatter.15.cloned.1.call-start = ((), (), s32[]{:S(2)}) async-start(), calls=%async_computation.15 | async-start | bytes 6684672 | tf_op jit(solution)/shard_map/reduce_scatter | solution.py:273
  653.4 119.6 %all-reduce.14.cloned.1.call-start = ((), (), s32[]{:S(2)}) async-start(), calls=%async_computation.24 | async-start | bytes 1327104 | tf_op jit(solution)/shard_map/psum | solution.py:344
  654.1 138.5 %reduce-scatter.23.cloned.1.call-start = ((), (), s32[]{:S(2)}) async-start(), calls=%async_computation.19 | async-start | bytes 1105920 | tf_op jit(solution)/shard_map/reduce_scatter | solution.py:322
  657.6 154.8 %reduce-scatter.17.cloned.1.call-start = ((), (), s32[]{:S(2)}) async-start(), calls=%async_computation.16 | async-start | bytes 1105920 | tf_op jit(solution)/shard_map/reduce_scatter | solution.py:313
  667.8 159.0 %reduce-scatter.21.cloned.1.call-start = ((), (), s32[]{:S(2)}) async-start(), calls=%async_computation.18 | async-start | bytes 442368 | tf_op jit(solution)/shard_map/reduce_scatter | solution.py:319
  740.6 101.0 %reduce-scatter.19.cloned.1.call-start = ((), (), s32[]{:S(2)}) async-start(), calls=%async_computation.17 | async-start | bytes 442368 | tf_op jit(solution)/shard_map/reduce_scatter | solution.py:316
  742.5 156.5 %reduce-scatter.11.cloned.1.call-start = ((), (), s32[]{:S(2)}) async-start(), calls=%async_computation.11 | async-start | bytes 3276800 | tf_op jit(solution)/shard_map/reduce_scatter | solution.py:196
  748.4 224.8 %all-reduce.12.cloned.1.call-start = ((), (), s32[]{:S(2)}) async-start(), calls=%async_computation.23 | async-start | bytes 2064384 | tf_op jit(solution)/shard_map/psum | solution.py:338
  783.3 58.4 %copy-start.57 = (bf16[576]{0:T(1024)(128)(2,1)S(1)}, bf16[576]{0:T(1024)(128)(2,1)}, u32[]{:S(2)}) copy-start(bf16[576]{0:T(1024)(128)(2,1)} %get-tuple-element.61) | copy-start | bytes 3460
  783.3 115.8 %copy-start.4 = (f32[8,64,576]{2,1,0:T(8,128)S(1)}, f32[8,64,576]{2,1,0:T(8,128)}, u32[]{:S(2)}) copy-start(f32[8,64,576]{2,1,0:T(8,128)} %copy-done.2) | copy-start | bytes 3538948
  783.3 115.8 %copy-start.46 = (f32[576]{0:T(1024)S(1)}, f32[576]{0:T(1024)}, u32[]{:S(2)}) copy-start(f32[576]{0:T(1024)} %copy-done.45) | copy-start | bytes 6916
  783.3 115.8 %copy-start.48 = (f32[8,64]{1,0:T(8,128)S(1)}, f32[8,64]{1,0:T(8,128)}, u32[]{:S(2)}) copy-start(f32[8,64]{1,0:T(8,128)} %copy-done.47) | copy-start | bytes 6148
  783.3 115.7 %copy-start.56 = (f32[8,64]{1,0:T(8,128)S(1)}, f32[8,64]{1,0:T(8,128)}, u32[]{:S(2)}) copy-start(f32[8,64]{1,0:T(8,128)} %copy-done.55) | copy-start | bytes 6148
  (41 other events, 470.4 us)
Sparse Core Ops, SparseCore 0:
  349.9 57.7 all-gather.3
  409.2 53.5 all-gather.5
  479.5 59.9 reduce-scatter.12
  542.1 14.1 reduce-scatter.28
  559.0 13.7 reduce-scatter.24
  575.5 13.7 reduce-scatter.26
  653.5 83.6 reduce-scatter.14
  739.7 33.2 all-reduce.13
  775.3 17.3 reduce-scatter.22
  795.4 16.9 reduce-scatter.16
  814.6 12.0 reduce-scatter.20
  829.4 12.1 reduce-scatter.18
  843.9 55.0 reduce-scatter.10
Sparse Core Ops, SparseCore 1:
  482.2 96.8 all-gather.7
  841.7 131.5 all-reduce.11
